TPU v7x, 128 devices: a whole 4x4x4 slice. The times are simulated.
128 devices in a mesh: seq: 32 (over y, x, z_lo), tp: 4 (over z_hi, core).
Axes of the slice: x: 4, y: 4, z: 4 (z_hi: 2, z_lo: 2; z = z_hi * 2 + z_lo), core: 2. Of those that a mesh axis runs over, the one named last changes fastest.
Arguments:
- hidden_in: bfloat16 [24576, 4096], P(('seq', 'tp')), may hold values from -26 to 26
- norm_gain: float32 [4096], replicated, may hold values from 0.1 to 1.9
- w_qkv: bfloat16 [3, 4096, 2048], P(None, None, 'tp'), may hold values from -1 to 1
- w_out: bfloat16 [2048, 4096], P('tp'), may hold values from -0.125 to 0.125
Outputs:
- datastore: bfloat16 [24576, 4096], P(('seq', 'tp'))
All inputs are finite; a program needn't handle non-finite values.
Results may differ from a plain program's by a relative error of at most 0.006.
Values may be sent and summed in bfloat16 or wider, within the bound.
A program may use at most 128 MiB of HBM per device.

v0:
```python
import jax
import jax.numpy as jnp
from jax import lax
from jax.sharding import PartitionSpec as P

HD = 64
SPAN = 512
epsilon = 1e-06


def extended(block, sides, width):
    for axis, dim in sides:
        count = lax.axis_size(axis)
        forward = [(i, i + 1) for i in range(count - 1)]
        backward = [(target, source) for source, target in forward]
        low = lax.ppermute(
            lax.slice_in_dim(block, block.shape[dim] - width, None, axis=dim), axis, forward
        )
        high = lax.ppermute(lax.slice_in_dim(block, 0, width, axis=dim), axis, backward)
        block = jnp.concatenate([low, block, high], axis=dim)
    return block


def rms_scale(rows_in, norm_gain):
    widened = rows_in.astype(jnp.float32)
    mean_square = jnp.mean(widened * widened, axis=1, keepdims=True)
    return (widened * lax.rsqrt(mean_square + epsilon) * norm_gain[None, :]).astype(jnp.bfloat16)


def attend(queries, keys_pad, values_pad, at_start, at_end):
    span_len = SPAN
    half_len = span_len // 2
    quarter = span_len // 4
    query_rows = queries.shape[0]
    block_count = query_rows // half_len
    head_count = queries.shape[1] // HD
    query_blocks = queries.reshape(block_count, half_len, head_count, HD)
    key_blocks = jnp.stack(
        [
            keys_pad[number * half_len : number * half_len + span_len]
            for number in range(block_count)
        ]
    )
    value_blocks = jnp.stack(
        [
            values_pad[number * half_len : number * half_len + span_len]
            for number in range(block_count)
        ]
    )
    key_blocks = key_blocks.reshape(block_count, span_len, head_count, HD)
    value_blocks = value_blocks.reshape(block_count, span_len, head_count, HD)
    scores = jnp.einsum(
        "bqhd,bkhd->bhqk", query_blocks, key_blocks, preferred_element_type=jnp.float32
    )
    key_place = (
        jnp.arange(block_count, dtype=jnp.int32)[:, None] * half_len
        + jnp.arange(span_len, dtype=jnp.int32)[None, :]
    )
    left_out = jnp.logical_and(at_start, key_place < quarter)
    right_out = jnp.logical_and(at_end, key_place >= query_rows + quarter)
    key_valid = jnp.logical_not(jnp.logical_or(left_out, right_out))
    scores = jnp.where(key_valid[:, None, None, :], scores, -1e30)
    row_max = jnp.max(scores, axis=-1, keepdims=True)
    powers = jnp.exp(scores - row_max)
    weights = (powers / jnp.sum(powers, axis=-1, keepdims=True)).astype(jnp.bfloat16)
    context = jnp.einsum(
        "bhqk,bkhd->bqhd", weights, value_blocks, preferred_element_type=jnp.float32
    )
    return context.astype(jnp.bfloat16).reshape(query_rows, head_count * HD)


def on_device(hidden_in, norm_gain, w_qkv, w_out):
    seq_count = lax.axis_size("seq")
    seq_index = lax.axis_index("seq")
    own_rows = hidden_in.shape[0]
    model_width = hidden_in.shape[1]
    inner_width = w_qkv.shape[2]
    quarter = SPAN // 4
    at_start = seq_index == 0
    at_end = seq_index == seq_count - 1
    normed = lax.all_gather(rms_scale(hidden_in, norm_gain), "tp", axis=0, tiled=True)
    queries = jnp.dot(normed, w_qkv[0], preferred_element_type=jnp.float32).astype(jnp.bfloat16)
    keys_own = jnp.dot(normed, w_qkv[1], preferred_element_type=jnp.float32).astype(jnp.bfloat16)
    values_own = jnp.dot(normed, w_qkv[2], preferred_element_type=jnp.float32).astype(jnp.bfloat16)
    joined = jnp.concatenate([keys_own, values_own], axis=1)
    padded = extended(joined, (("seq", 0),), quarter)
    keys_pad = padded[:, :inner_width]
    values_pad = padded[:, inner_width:]
    context = attend(queries, keys_pad, values_pad, at_start, at_end)
    own_sum = lax.psum_scatter(
        jnp.dot(context, w_out, preferred_element_type=jnp.float32).astype(jnp.bfloat16),
        "tp",
        scatter_dimension=0,
        tiled=True,
    ).astype(jnp.float32)
    new_state = (hidden_in.astype(jnp.float32) + own_sum).astype(jnp.bfloat16)
    stripe_len = own_rows // seq_count
    pieces = new_state.reshape(seq_count, stripe_len, model_width)
    received = lax.all_to_all(pieces, "seq", split_axis=0, concat_axis=0, tiled=True)
    return received.reshape(own_rows, model_width)


def solution(mesh):
    return jax.shard_map(
        on_device,
        mesh=mesh,
        in_specs=(P(("seq", "tp"), None), P(), P(None, None, "tp"), P("tp", None)),
        out_specs=P(("seq", "tp"), None),
        check_vma=False,
    )
```

profile of v0, /device:TPU:0, one launch (start us, length us, event | category | flops | bytes accessed | tf_op | source)
XLA Modules:
  0.0 249.0 jit_solution(113620848852326442)
XLA Ops:
  6.5 1.8 fusion.16
  8.3 3.0 %fusion.18 = bf16[192,4096]{1,0:T(8,128)(2,1)} fusion(bf16[192,4096]{1,0:T(8,128)(2,1)} %param.4, f32[4096]{0:T(1024)} %param.5, f32[192]{0:T(256)S(1)} %add_rsqrt_fusion), kind=kLoop, calls=%fused_computation.23 | loop fusion | flops 3145728 | bytes 3162880 | tf_op jit(solution)/shard_map/convert_element_type | solution.py:27
  11.5 0.1 fusion.52
  11.6 53.0 %all-gather.2.cloned.1.call-done = bf16[768,4096]{1,0:T(8,128)(2,1)} async-done(((bf16[192,4096]{1,0:T(8,128)(2,1)}), bf16[768,4096]{1,0:T(8,128)(2,1)}) %all-gather.2.cloned.1.call-update) | async-done | bytes 6291472 | tf_op jit(solution)/shard_map/all_gather | solution.py:81
  64.6 7.6 %fusion.35 = bf16[768,512]{0,1:T(8,128)(2,1)S(1)} fusion(bf16[768,4096]{1,0:T(8,128)(2,1)} %all-gather.2.cloned.1.call-done, bf16[3,4096,512]{2,1,0:T(8,128)(2,1)} %param.6), kind=kOutput, calls=%fused_computation.38 | convolution fusion | flops 3221618688 | bytes 11272192 | tf_op jit(solution)/shard_map/dot_general | solution.py:84
  72.2 5.9 %fusion.32 = bf16[768,512]{0,1:T(8,128)(2,1)S(1)} fusion(bf16[768,4096]{1,0:T(8,128)(2,1)S(1)} %copy-done.4, bf16[3,4096,512]{2,1,0:T(8,128)(2,1)} %param.6), kind=kOutput, calls=%fused_computation.37 | convolution fusion | flops 3221618688 | bytes 11272192 | tf_op jit(solution)/shard_map/dot_general | solution.py:83
  78.1 0.8 pad_maximum_fusion.7
  79.0 2.6 %collective-permute-start = (bf16[128,1024]{0,1:T(8,128)(2,1)}, bf16[128,1024]{0,1:T(8,128)(2,1)S(1)}, u32[]{:S(2)}, u32[]{:S(2)}) collective-permute-start(bf16[128,1024]{0,1:T(8,128)(2,1)} %get-tuple-element.11), channel_id=1, source_target_pairs={{0,4},{4,8},{8,12},{12,16},{16,20},{20,24},{24,28},{28,32},{32,36}... | collective-permute-start | bytes 786440 | tf_op jit(solution)/shard_map/ppermute | solution.py:16
  81.5 1.3 collective-permute-start.1
  82.8 6.5 %fusion.38 = bf16[768,512]{1,0:T(8,128)(2,1)} fusion(bf16[768,4096]{1,0:T(8,128)(2,1)S(1)} %copy-done.4, bf16[3,4096,512]{2,1,0:T(8,128)(2,1)} %param.6), kind=kOutput, calls=%fused_computation.39 | convolution fusion | flops 3221618688 | bytes 11272192 | tf_op jit(solution)/shard_map/dot_general | solution.py:82
  89.3 2.4 reshape.69
  91.8 1.6 collective-permute-done
  93.4 2.2 pad_maximum_fusion.5
  95.6 6.3 %fusion.25 = f32[3,8,256,512]{3,2,1,0:T(8,128)} fusion(bf16[1,512,8,64]{1,3,2,0:T(8,128)(2,1)S(1)} %bitcast.35, bf16[1,512,8,64]{1,3,2,0:T(8,128)(2,1)S(1)} %bitcast.36, bf16[1,512,8,64]{1,3,2,0:T(8,128)(2,1)S(1)} %bitcast.34, bf16[3,256,8,64]{3,2,1,0:T(8,128)(2,1)S(1)} %reshape.69), kind=kOutput, calls=%fused_computation.30 | convolution fusion | flops 404226048 | bytes 14942208 | tf_op jit(solution)/shard_map/bqhd,bkhd->bhqk/dot_general | solution.py:52
  101.9 15.4 %fusion.56 = (f32[3,8,256]{2,1,0:T(8,128)S(1)}, f32[3,8,256,512]{3,2,1,0:T(8,128)}) fusion(f32[3,8,256,512]{3,2,1,0:T(8,128)} %fusion.25, pred[3,512]{1,0:T(4,128)(4,1)S(1)} %fusion.52), kind=kOutput, calls=%fused_computation.62 | output fusion | flops 12583423 | bytes 25191936 | tf_op jit(solution)/shard_map/sub | solution.py:64
  117.3 6.0 %fusion.44 = bf16[3,256,8,64]{1,3,2,0:T(8,128)(2,1)S(1)} fusion(f32[3,8,256,512]{3,2,1,0:T(8,128)} %get-tuple-element.16, f32[3,8,256]{2,1,0:T(8,128)S(1)} %get-tuple-element.15, bf16[1,512,8,64]{1,3,2,0:T(8,128)(2,1)S(1)} %bitcast.39, bf16[1,512,8,64]{1,3,2,0:T(8,128)(2,1)S(1)} %bitcast.40, bf16[1,512,8,64]{1,3,2,0:T(8,128)(2,1)S(1)} %bitcast.38), kind=kOutput, calls=%fused_computation.41 | convolution fusion | flops 410910720 | bytes 14966784 | tf_op jit(solution)/shard_map/bhqk,bkhd->bqhd/dot_general | solution.py:66
  123.3 0.7 copy.8
  123.9 0.2 copy.11
  124.1 5.4 %convolution_convert_fusion = bf16[768,4096]{1,0:T(8,128)(2,1)} fusion(bf16[768,512]{0,1:T(8,128)(2,1)S(1)} %bitcast.37, bf16[512,4096]{1,0:T(8,128)(2,1)S(1)} %copy-done.5), kind=kOutput, calls=%fused_computation.5 | convolution fusion | flops 3224371200 | bytes 11272192 | tf_op jit(solution)/shard_map/dot_general | solution.py:91
  129.5 67.5 %reduce-scatter.2.cloned.1.call-done = bf16[192,4096]{1,0:T(8,128)(2,1)} async-done(((bf16[768,4096]{1,0:T(8,128)(2,1)}), bf16[192,4096]{1,0:T(8,128)(2,1)}) %reduce-scatter.2.cloned.1.call-update) | async-done | bytes 1572880 | tf_op jit(solution)/shard_map/reduce_scatter | solution.py:90
  197.0 3.1 %fusion.19 = bf16[192,4096]{1,0:T(8,128)(2,1)} fusion(bf16[192,4096]{1,0:T(8,128)(2,1)S(1)} %copy-done, bf16[192,4096]{1,0:T(8,128)(2,1)} %reduce-scatter.2.cloned.1.call-done), kind=kLoop, calls=%fused_computation.24 | loop fusion | flops 3145728 | bytes 4718592 | tf_op jit(solution)/shard_map/convert_element_type | solution.py:96
  200.1 2.4 reshape.67
  202.5 36.0 %all_to_all.5 = bf16[32,6,4096]{2,1,0:T(8,128)(2,1)} all-to-all(bf16[32,6,4096]{2,1,0:T(8,128)(2,1)S(1)} %reshape.67), channel_id=1, replica_groups=mesh['seq'=32,'tp'=4] {'seq'}, dimensions={0} | all-to-all | bytes 3145728 | tf_op jit(solution)/shard_map/all_to_all | solution.py:99
  238.5 3.7 %reshape.68 = bf16[192,4096]{1,0:T(8,128)(2,1)} reshape(bf16[32,6,4096]{2,1,0:T(8,128)(2,1)} %all_to_all.5) | data formatting | bytes 3145728 | tf_op jit(solution)/shard_map/reshape | solution.py:100
  (19 shorter events, 0.1 us)
Async XLA Ops:
  6.5 58.1 %all-gather.2.cloned.1.call-start = ((), (), s32[]{:S(2)}) async-start(), calls=%async_computation.2 | async-start | bytes 7864320 | tf_op jit(solution)/shard_map/all_gather | solution.py:81
  11.4 185.6 %reduce-scatter.2.cloned.1.call-start = ((), (), s32[]{:S(2)}) async-start(), calls=%async_computation.3 | async-start | bytes 7864320 | tf_op jit(solution)/shard_map/reduce_scatter | solution.py:90
  64.6 7.6 %copy-start.4 = (bf16[768,4096]{1,0:T(8,128)(2,1)S(1)}, bf16[768,4096]{1,0:T(8,128)(2,1)}, u32[]{:S(2)}) copy-start(bf16[768,4096]{1,0:T(8,128)(2,1)} %all-gather.2.cloned.1.call-done) | copy-start | bytes 18874372
  79.0 14.5 %collective-permute-start = (bf16[128,1024]{0,1:T(8,128)(2,1)}, bf16[128,1024]{0,1:T(8,128)(2,1)S(1)}, u32[]{:S(2)}, u32[]{:S(2)}) collective-permute-start(bf16[128,1024]{0,1:T(8,128)(2,1)} %get-tuple-element.11), channel_id=1, source_target_pairs={{0,4},{4,8},{8,12},{12,16},{16,20},{20,24},{24,28},{28,32},{32,36}... | collective-permute-start | bytes 786440 | tf_op jit(solution)/shard_map/ppermute | solution.py:16
  81.5 11.9 %collective-permute-start.1 = (bf16[128,1024]{0,1:T(8,128)(2,1)}, bf16[128,1024]{0,1:T(8,128)(2,1)}, u32[]{:S(2)}, u32[]{:S(2)}) collective-permute-start(bf16[128,1024]{0,1:T(8,128)(2,1)} %get-tuple-element.12), channel_id=1, source_target_pairs={{4,0},{8,4},{12,8},{16,12},{20,16},{24,20},{28,24},{32,28},{36,32}... | collective-permute-start | bytes 786440 | tf_op jit(solution)/shard_map/ppermute | solution.py:19
  101.9 15.4 %copy-start.1 = (bf16[512,512]{0,1:T(8,128)(2,1)S(1)}, bf16[512,512]{0,1:T(8,128)(2,1)}, u32[]{:S(2)}) copy-start(bf16[512,512]{0,1:T(8,128)(2,1)} %get-tuple-element.5) | copy-start | bytes 1572868
  101.9 15.4 %copy-start.2 = (bf16[512,512]{0,1:T(8,128)(2,1)S(1)}, bf16[512,512]{0,1:T(8,128)(2,1)}, u32[]{:S(2)}) copy-start(bf16[512,512]{0,1:T(8,128)(2,1)} %get-tuple-element.10) | copy-start | bytes 1572868
  101.9 15.4 %copy-start.3 = (bf16[512,512]{0,1:T(8,128)(2,1)S(1)}, bf16[512,512]{0,1:T(8,128)(2,1)}, u32[]{:S(2)}) copy-start(bf16[512,512]{0,1:T(8,128)(2,1)} %get-tuple-element.14) | copy-start | bytes 1572868
  117.3 6.8 %copy-start.5 = (bf16[512,4096]{1,0:T(8,128)(2,1)S(1)}, bf16[512,4096]{1,0:T(8,128)(2,1)}, u32[]{:S(2)}) copy-start(bf16[512,4096]{1,0:T(8,128)(2,1)} %param.7) | copy-start | bytes 12582916
  129.5 67.5 %copy-start = (bf16[192,4096]{1,0:T(8,128)(2,1)S(1)}, bf16[192,4096]{1,0:T(8,128)(2,1)}, u32[]{:S(2)}) copy-start(bf16[192,4096]{1,0:T(8,128)(2,1)} %param.4) | copy-start | bytes 4718596
Sparse Core Ops, SparseCore 0:
  11.5 53.0 all-gather.1
  129.6 67.2 reduce-scatter.1
where the time goes:
time: 250 us; the launch traced here: 249 us
  waiting for transfers between devices  122 us (49%)
  matrix products  37.6 us (15%)
  blocking collectives  36 us (14%)
  other arithmetic  26.4 us (11%)
  between operations  13.5 us (5%)
  local copies, waits for them, and re-layouts  9.4 us (4%)
  starting transfers between devices  3.9 us (2%)
    reduce_scatter x1, waiting for transfers between devices, on_device(): lax.psum_scatter(jnp.dot(context, w_out, preferred_element_type=jnp.float...  67.5 us
    all_gather x1, waiting for transfers between devices, on_device(): lax.all_gather(rms_scale(hidden_in, norm_gain), 'tp', axis=0, tiled=True)  53 us
    all_to_all x1, blocking collectives, on_device(): lax.all_to_all(pieces, 'seq', split_axis=0, concat_axis=0, tiled=True)  36 us
    sub x1, other arithmetic, attend(): powers = jnp.exp(scores - row_max)  15.4 us
    dot_general x1, matrix products, on_device(): jnp.dot(normed, w_qkv[2], preferred_element_type=jnp.float32)  7.61 us
    dot_general x1, matrix products, on_device(): jnp.dot(normed, w_qkv[0], preferred_element_type=jnp.float32)  6.49 us
    dot_general x1, matrix products, attend(): jnp.einsum('bqhd,bkhd->bhqk', query_blocks, key_blocks, preferred_element...  6.26 us
    dot_general x1, matrix products, attend(): jnp.einsum('bhqk,bkhd->bqhd', weights, value_blocks, preferred_element_ty...  5.96 us
  transfers between devices with their start and end apart: 4, of which 3 were waited for; matrix products, arithmetic and copies ran while one was open for 4% of the time, Pallas kernels for 0%

commit v1 on v0

--- a/solution.py
+++ b/solution.py
@@ -78,7 +78,11 @@
     quarter = SPAN // 4
     at_start = seq_index == 0
     at_end = seq_index == seq_count - 1
-    normed = lax.all_gather(rms_scale(hidden_in, norm_gain), "tp", axis=0, tiled=True)
+    own = rms_scale(hidden_in, norm_gain)
+    n_dev = lax.axis_size("tp")
+    shards = jnp.stack([own for _ in range(n_dev)])
+    shards = lax.all_to_all(shards, "tp", split_axis=0, concat_axis=0)
+    normed = jnp.concatenate(shards, axis=0)
     queries = jnp.dot(normed, w_qkv[0], preferred_element_type=jnp.float32).astype(jnp.bfloat16)
     keys_own = jnp.dot(normed, w_qkv[1], preferred_element_type=jnp.float32).astype(jnp.bfloat16)
     values_own = jnp.dot(normed, w_qkv[2], preferred_element_type=jnp.float32).astype(jnp.bfloat16)

time: 250 us -> 279 us (1.12)
  waiting for transfers between devices: 122 us -> 139 us
  starting transfers between devices: 3.9 us -> 10.4 us
  local copies, waits for them, and re-layouts: 9.4 us -> 12.8 us
  matrix products: 37.6 us -> 40.8 us
    all_to_all x0 -> x1, waiting for transfers between devices: none -> 72.2 us  [on_device(): shards = lax.all_to_all(shards, 'tp', split_axis=0, concat_axis=0)]
    all_gather x1 -> x0, waiting for transfers between devices: 53 us -> none  [on_device(): lax.all_gather(rms_scale(hidden_in, norm_gain), 'tp', axis=0, tiled=True)]
    all_to_all x0 -> x1, starting transfers between devices: none -> 5.26 us  [on_device(): shards = lax.all_to_all(shards, 'tp', split_axis=0, concat_axis=0)]
    another operation x0 -> x1, local copies, waits for them, and re-layouts: none -> 3.43 us  [on_device(): shards = jnp.stack([own for _ in range(n_dev)])]
  transfers between devices with their start and end apart: 4 -> 4, of which waited for: 3 -> 2; matrix products, arithmetic and copies ran while one was open for 4% -> 4% of each run, Pallas kernels for 0% -> 0%
where the time goes in v1:
time: 279 us; the launch traced here: 278 us
  waiting for transfers between devices  139 us (50%)
  matrix products  40.8 us (15%)
  blocking collectives  36 us (13%)
  other arithmetic  25.3 us (9%)
  between operations  13.5 us (5%)
  local copies, waits for them, and re-layouts  12.8 us (5%)
  starting transfers between devices  10.4 us (4%)
    all_to_all x1, waiting for transfers between devices, on_device(): shards = lax.all_to_all(shards, 'tp', split_axis=0, concat_axis=0)  72.2 us
    reduce_scatter x1, waiting for transfers between devices, on_device(): lax.psum_scatter(jnp.dot(context, w_out, preferred_element_type=jnp.float...  67.3 us
    all_to_all x1, blocking collectives, on_device(): lax.all_to_all(pieces, 'seq', split_axis=0, concat_axis=0, tiled=True)  36 us
    sub x1, other arithmetic, attend(): powers = jnp.exp(scores - row_max)  15.4 us
    dot_general x1, matrix products, on_device(): jnp.dot(normed, w_qkv[0], preferred_element_type=jnp.float32)  8.29 us
    dot_general x1, matrix products, on_device(): jnp.dot(normed, w_qkv[1], preferred_element_type=jnp.float32)  7.47 us
    dot_general x1, matrix products, on_device(): jnp.dot(normed, w_qkv[2], preferred_element_type=jnp.float32)  7.47 us
    dot_general x1, matrix products, attend(): jnp.einsum('bqhd,bkhd->bhqk', query_blocks, key_blocks, preferred_element...  6.25 us
  transfers between devices with their start and end apart: 4, of which 2 were waited for; matrix products, arithmetic and copies ran while one was open for 4% of the time, Pallas kernels for 0%

profile of v1, /device:TPU:0, one launch (start us, length us, event | category | flops | bytes accessed | tf_op | source)
XLA Modules:
  0.0 278.3 jit_solution(442021781067473934)
XLA Ops:
  6.5 1.8 fusion.16
  8.3 1.9 fusion.18
  10.2 3.4 %stack.31 = bf16[4,192,4096]{2,1,0:T(8,128)(2,1)} broadcast(bf16[192,4096]{1,0:T(8,128)(2,1)S(1)} %fusion.18), dimensions={1,2} | broadcast | bytes 7864320 | tf_op jit(solution)/shard_map/stack | solution.py:83
  13.7 5.3 %all-to-all-start = ((bf16[4,192,4096]{2,1,0:T(8,128)(2,1)}), bf16[4,192,4096]{2,1,0:T(8,128)(2,1)}, u32[]{:S(2)}, u32[]{:S(2)}) async-start(bf16[4,192,4096]{2,1,0:T(8,128)(2,1)} %stack.31), calls=%async_computation | async-start | bytes 12582912 | tf_op jit(solution)/shard_map/all_to_all | solution.py:84
  19.1 72.2 %all-to-all-done = bf16[4,192,4096]{2,1,0:T(8,128)(2,1)} async-done(((bf16[4,192,4096]{2,1,0:T(8,128)(2,1)}), bf16[4,192,4096]{2,1,0:T(8,128)(2,1)}, u32[]{:S(2)}, u32[]{:S(2)}) %all-to-all-start) | async-done | bytes 6291488 | tf_op jit(solution)/shard_map/all_to_all | solution.py:84
  91.3 7.5 %fusion.35 = bf16[768,512]{0,1:T(8,128)(2,1)S(1)} fusion(bf16[768,4096]{1,0:T(8,128)(2,1)} %bitcast, bf16[3,4096,512]{2,1,0:T(8,128)(2,1)} %param.6), kind=kOutput, calls=%fused_computation.38 | convolution fusion | flops 3221618688 | bytes 11272192 | tf_op jit(solution)/shard_map/dot_general | solution.py:88
  98.7 7.5 %fusion.32 = bf16[768,512]{0,1:T(8,128)(2,1)S(1)} fusion(bf16[768,4096]{1,0:T(8,128)(2,1)} %bitcast, bf16[3,4096,512]{2,1,0:T(8,128)(2,1)} %param.6), kind=kOutput, calls=%fused_computation.37 | convolution fusion | flops 3221618688 | bytes 11272192 | tf_op jit(solution)/shard_map/dot_general | solution.py:87
  106.2 0.8 pad_maximum_fusion.7
  107.1 3.8 %collective-permute-start = (bf16[128,1024]{0,1:T(8,128)(2,1)}, bf16[128,1024]{0,1:T(8,128)(2,1)S(1)}, u32[]{:S(2)}, u32[]{:S(2)}) collective-permute-start(bf16[128,1024]{0,1:T(8,128)(2,1)} %get-tuple-element.11), channel_id=1, source_target_pairs={{0,4},{4,8},{8,12},{12,16},{16,20},{20,24},{24,28},{28,32},{32,36}... | collective-permute-start | bytes 786440 | tf_op jit(solution)/shard_map/ppermute | solution.py:16
  110.8 1.3 collective-permute-start.1
  112.1 8.3 %fusion.38 = bf16[768,512]{1,0:T(8,128)(2,1)} fusion(bf16[768,4096]{1,0:T(8,128)(2,1)} %bitcast, bf16[3,4096,512]{2,1,0:T(8,128)(2,1)} %param.6), kind=kOutput, calls=%fused_computation.39 | convolution fusion | flops 3221618688 | bytes 11272192 | tf_op jit(solution)/shard_map/dot_general | solution.py:86
  120.4 2.4 reshape.75
  122.9 2.2 pad_maximum_fusion.5
  125.1 6.3 %fusion.25 = f32[3,8,256,512]{3,2,1,0:T(8,128)} fusion(bf16[1,512,8,64]{1,3,2,0:T(8,128)(2,1)S(1)} %bitcast.36, bf16[1,512,8,64]{1,3,2,0:T(8,128)(2,1)S(1)} %bitcast.37, bf16[1,512,8,64]{1,3,2,0:T(8,128)(2,1)S(1)} %bitcast.35, bf16[3,256,8,64]{3,2,1,0:T(8,128)(2,1)S(1)} %reshape.75), kind=kOutput, calls=%fused_computation.30 | convolution fusion | flops 404226048 | bytes 14942208 | tf_op jit(solution)/shard_map/bqhd,bkhd->bhqk/dot_general | solution.py:52
  131.4 15.4 %fusion.56 = (f32[3,8,256]{2,1,0:T(8,128)S(1)}, f32[3,8,256,512]{3,2,1,0:T(8,128)}) fusion(f32[3,8,256,512]{3,2,1,0:T(8,128)} %fusion.25, pred[3,512]{1,0:T(4,128)(4,1)S(1)} %fusion.52), kind=kOutput, calls=%fused_computation.62 | output fusion | flops 12583423 | bytes 25191936 | tf_op jit(solution)/shard_map/sub | solution.py:64
  146.8 6.0 %fusion.44 = bf16[3,256,8,64]{1,3,2,0:T(8,128)(2,1)S(1)} fusion(f32[3,8,256,512]{3,2,1,0:T(8,128)} %get-tuple-element.16, f32[3,8,256]{2,1,0:T(8,128)S(1)} %get-tuple-element.15, bf16[1,512,8,64]{1,3,2,0:T(8,128)(2,1)S(1)} %bitcast.40, bf16[1,512,8,64]{1,3,2,0:T(8,128)(2,1)S(1)} %bitcast.41, bf16[1,512,8,64]{1,3,2,0:T(8,128)(2,1)S(1)} %bitcast.39), kind=kOutput, calls=%fused_computation.41 | convolution fusion | flops 410910720 | bytes 14966784 | tf_op jit(solution)/shard_map/bhqk,bkhd->bqhd/dot_general | solution.py:66
  152.8 0.7 copy.8
  153.4 0.2 copy.11
  153.6 5.4 %convolution_convert_fusion = bf16[768,4096]{1,0:T(8,128)(2,1)} fusion(bf16[768,512]{0,1:T(8,128)(2,1)S(1)} %bitcast.38, bf16[512,4096]{1,0:T(8,128)(2,1)S(1)} %copy-done.4), kind=kOutput, calls=%fused_computation.5 | convolution fusion | flops 3224371200 | bytes 11272192 | tf_op jit(solution)/shard_map/dot_general | solution.py:95
  159.0 67.3 %reduce-scatter.2.cloned.1.call-done = bf16[192,4096]{1,0:T(8,128)(2,1)} async-done(((bf16[768,4096]{1,0:T(8,128)(2,1)}), bf16[192,4096]{1,0:T(8,128)(2,1)}) %reduce-scatter.2.cloned.1.call-update) | async-done | bytes 1572880 | tf_op jit(solution)/shard_map/reduce_scatter | solution.py:94
  226.3 3.1 %fusion.19 = bf16[192,4096]{1,0:T(8,128)(2,1)} fusion(bf16[192,4096]{1,0:T(8,128)(2,1)S(1)} %copy-done, bf16[192,4096]{1,0:T(8,128)(2,1)} %reduce-scatter.2.cloned.1.call-done), kind=kLoop, calls=%fused_computation.24 | loop fusion | flops 3145728 | bytes 4718592 | tf_op jit(solution)/shard_map/convert_element_type | solution.py:100
  229.4 2.4 reshape.73
  231.8 36.0 %all_to_all.10 = bf16[32,6,4096]{2,1,0:T(8,128)(2,1)} all-to-all(bf16[32,6,4096]{2,1,0:T(8,128)(2,1)S(1)} %reshape.73), channel_id=1, replica_groups=mesh['seq'=32,'tp'=4] {'seq'}, dimensions={0} | all-to-all | bytes 3145728 | tf_op jit(solution)/shard_map/all_to_all | solution.py:103
  267.8 3.7 %reshape.74 = bf16[192,4096]{1,0:T(8,128)(2,1)} reshape(bf16[32,6,4096]{2,1,0:T(8,128)(2,1)} %all_to_all.10) | data formatting | bytes 3145728 | tf_op jit(solution)/shard_map/reshape | solution.py:104
  (17 shorter events, 0.2 us)
Async XLA Ops:
  13.7 77.6 %all-to-all-start = ((bf16[4,192,4096]{2,1,0:T(8,128)(2,1)}), bf16[4,192,4096]{2,1,0:T(8,128)(2,1)}, u32[]{:S(2)}, u32[]{:S(2)}) async-start(bf16[4,192,4096]{2,1,0:T(8,128)(2,1)} %stack.31), calls=%async_computation | async-start | bytes 12582912 | tf_op jit(solution)/shard_map/all_to_all | solution.py:84
  18.9 207.4 %reduce-scatter.2.cloned.1.call-start = ((), (), s32[]{:S(2)}) async-start(), calls=%async_computation.3 | async-start | bytes 7864320 | tf_op jit(solution)/shard_map/reduce_scatter | solution.py:94
  107.1 15.8 %collective-permute-start = (bf16[128,1024]{0,1:T(8,128)(2,1)}, bf16[128,1024]{0,1:T(8,128)(2,1)S(1)}, u32[]{:S(2)}, u32[]{:S(2)}) collective-permute-start(bf16[128,1024]{0,1:T(8,128)(2,1)} %get-tuple-element.11), channel_id=1, source_target_pairs={{0,4},{4,8},{8,12},{12,16},{16,20},{20,24},{24,28},{28,32},{32,36}... | collective-permute-start | bytes 786440 | tf_op jit(solution)/shard_map/ppermute | solution.py:16
  110.8 12.1 %collective-permute-start.1 = (bf16[128,1024]{0,1:T(8,128)(2,1)}, bf16[128,1024]{0,1:T(8,128)(2,1)}, u32[]{:S(2)}, u32[]{:S(2)}) collective-permute-start(bf16[128,1024]{0,1:T(8,128)(2,1)} %get-tuple-element.12), channel_id=1, source_target_pairs={{4,0},{8,4},{12,8},{16,12},{20,16},{24,20},{28,24},{32,28},{36,32}... | collective-permute-start | bytes 786440 | tf_op jit(solution)/shard_map/ppermute | solution.py:19
  131.4 15.4 %copy-start.1 = (bf16[512,512]{0,1:T(8,128)(2,1)S(1)}, bf16[512,512]{0,1:T(8,128)(2,1)}, u32[]{:S(2)}) copy-start(bf16[512,512]{0,1:T(8,128)(2,1)} %get-tuple-element.5) | copy-start | bytes 1572868
  131.4 15.4 %copy-start.2 = (bf16[512,512]{0,1:T(8,128)(2,1)S(1)}, bf16[512,512]{0,1:T(8,128)(2,1)}, u32[]{:S(2)}) copy-start(bf16[512,512]{0,1:T(8,128)(2,1)} %get-tuple-element.10) | copy-start | bytes 1572868
  131.4 15.4 %copy-start.3 = (bf16[512,512]{0,1:T(8,128)(2,1)S(1)}, bf16[512,512]{0,1:T(8,128)(2,1)}, u32[]{:S(2)}) copy-start(bf16[512,512]{0,1:T(8,128)(2,1)} %get-tuple-element.14) | copy-start | bytes 1572868
  146.8 6.8 %copy-start.4 = (bf16[512,4096]{1,0:T(8,128)(2,1)S(1)}, bf16[512,4096]{1,0:T(8,128)(2,1)}, u32[]{:S(2)}) copy-start(bf16[512,4096]{1,0:T(8,128)(2,1)} %param.7) | copy-start | bytes 12582916
  159.0 67.3 %copy-start = (bf16[192,4096]{1,0:T(8,128)(2,1)S(1)}, bf16[192,4096]{1,0:T(8,128)(2,1)}, u32[]{:S(2)}) copy-start(bf16[192,4096]{1,0:T(8,128)(2,1)} %param.4) | copy-start | bytes 4718596
Sparse Core Ops, SparseCore 0:
  159.1 67.1 reduce-scatter.1
